TPU v7x, 128 devices: a whole 4x4x4 slice. The times are simulated.
128 devices in a mesh: dp: 32 (over x, y, core), tensor: 4 (over z).
Axes of the slice: x: 4, y: 4, z: 4, core: 2. Of those that a mesh axis runs over, the one named last changes fastest.
Arguments:
- activations: bfloat16 [32, 1536, 2048], P('dp', 'tensor'), may hold values from -6 to 6
- upstream_grad: bfloat16 [32, 1536, 4096], P('dp', None, 'tensor'), may hold values from -0.15625 to 0.15625
- feedback: bfloat16 [32, 2048, 4096], P('dp', None, 'tensor'), may hold values from -3 to 3
- selected: int32 [32, 4, 2], P('dp', 'tensor'), may hold values from -1 to 255, as said below
- cycle_values: bfloat16 [8, 4, 64, 64, 128], P(None, 'tensor'), may hold values from -6 to 6
- cycle_blocks: int32 [8, 4, 64], P(None, 'tensor'), may hold values from -1 to 255, as said below
- cycle_position: int32 [1], replicated, may hold values from 0 to 7
Outputs:
- update_dir: bfloat16 [2048, 4096], P(None, 'tensor')
- new_feedback: bfloat16 [32, 2048, 4096], P('dp', None, 'tensor')
- newest_values: bfloat16 [4, 64, 64, 128], P('tensor')
Inputs may be any that keep to these rules, and one draw needn't show every extreme that they name: `selected`: for each replica and tensor shard, the 2 entries hold 1 to 2 distinct block numbers first, then -1; in every tensor shard some replica lists 2 blocks. `cycle_blocks`: within each slot and tensor shard, entries r * 2 to r * 2 + 1 hold 1 to 2 distinct block numbers first, then -1; in every slot and shard some group of 2 entries is full.
All inputs are finite; a program needn't handle non-finite values.
Results may differ from a plain program's by a relative error of at most 0.0023.
Values may be sent and summed in bfloat16 or wider, within the bound.
No kernel may reach another device: no remote copies, remote signals or barrier semaphores. Data moves between devices by JAX's collectives and lax.ppermute only.
A program may use at most 192 MiB of HBM per device.

v0:
```python
import jax
import jax.numpy as jnp
from jax import lax
from jax.sharding import PartitionSpec as P

D = 2048
BH = 64
BW = 128
SLOTS = 8
decay_first = 0.9
decay_second = 0.999
epsilon = 0.001


def to_blocks(matrix):
    row_blocks = matrix.shape[0] // BH
    col_blocks = matrix.shape[1] // BW
    return (
        matrix.reshape(row_blocks, BH, col_blocks, BW)
        .transpose(0, 2, 1, 3)
        .reshape(row_blocks * col_blocks, BH, BW)
    )


def from_blocks(blocks, height, breadth):
    return (
        blocks.reshape(height // BH, breadth // BW, BH, BW)
        .transpose(0, 2, 1, 3)
        .reshape(height, breadth)
    )


def local(
    activations, upstream_grad, feedback, selected, cycle_values, cycle_blocks, cycle_position
):
    token_rows = activations[0]
    upstream = upstream_grad[0]
    shard_width = upstream.shape[1]
    contract = (((0,), (0,)), ((), ()))
    gathered = lax.all_gather(token_rows, "tensor", axis=0, tiled=True)
    gradient = lax.dot_general(gathered, upstream, contract, preferred_element_type=jnp.float32)
    accumulated = gradient + feedback[0].astype(jnp.float32)
    blocks = to_blocks(accumulated)
    block_total = blocks.shape[0]
    chosen = selected[0, 0]
    is_live = chosen >= 0
    safe_index = jnp.where(is_live, chosen, 0)
    outgoing = (blocks[safe_index] * is_live[:, None, None]).astype(jnp.bfloat16)
    cleared = jnp.any(jnp.arange(block_total)[:, None] == chosen[None, :], axis=1)
    remaining = jnp.where(cleared[:, None, None], 0.0, blocks)
    new_feedback = from_blocks(remaining, D, shard_width).astype(jnp.bfloat16)[None]
    all_values, all_blocks = (
        lax.all_gather(outgoing, "dp", axis=0, tiled=True),
        lax.all_gather(chosen, "dp", axis=0, tiled=True),
    )
    entry_total = all_values.shape[0]
    position = cycle_position[0]
    targets = jnp.arange(block_total)
    first_moment = jnp.zeros((block_total, BH * BW), jnp.float32)
    second_moment = jnp.zeros((block_total, BH * BW), jnp.float32)
    for slot_number in range(SLOTS):
        newest = position == slot_number
        values = jnp.where(newest, all_values, cycle_values[slot_number, 0])
        listed = jnp.where(newest, all_blocks, cycle_blocks[slot_number, 0])
        onehot = (targets[:, None] == listed[None, :]).astype(jnp.bfloat16)
        densified = jnp.dot(
            onehot, values.reshape(entry_total, BH * BW), preferred_element_type=jnp.float32
        )
        slot_age = jnp.mod(position - slot_number, SLOTS).astype(jnp.float32)
        weight_first = (1.0 - decay_first) * jnp.power(decay_first, slot_age)
        weight_second = (1.0 - decay_second) * jnp.power(decay_second, slot_age)
        first_moment = first_moment + weight_first * densified
        second_moment = second_moment + weight_second * (densified * densified)
    update = (
        (first_moment / (jnp.sqrt(second_moment) + epsilon))
        .astype(jnp.bfloat16)
        .reshape(block_total, BH, BW)
    )
    update_dir = from_blocks(update, D, shard_width)
    return (update_dir, new_feedback, all_values[None])


def solution(mesh):
    placed = (
        P("dp", "tensor", None),
        P("dp", None, "tensor"),
        P("dp", None, "tensor"),
        P("dp", "tensor", None),
        P(None, "tensor", None, None, None),
        P(None, "tensor", None),
        P(),
    )
    return jax.shard_map(
        local,
        mesh=mesh,
        in_specs=placed,
        out_specs=(P(None, "tensor"), P("dp", None, "tensor"), P("tensor", None, None, None)),
        check_vma=False,
    )
```

profile of v0, /device:TPU:1, one launch (start us, length us, event | category | flops | bytes accessed | tf_op | source)
XLA Modules:
  0.0 211.0 jit_solution(4553705174519842768)
XLA Ops:
  7.2 0.0 copy-start
  7.2 0.0 all-gather.7.cloned.1.call-start
  7.2 0.7 all-gather.7.cloned.1.call-update
  7.9 0.0 all-gather.5.cloned.1.call-start
  8.0 0.9 compare_reduce_fusion
  8.9 0.1 broadcast_in_dim.20
  9.0 0.7 fusion.44
  9.6 0.7 compare_convert_fusion
  10.3 68.5 %all-gather.7.cloned.1.call-done = bf16[1,1536,2048]{2,1,0:T(8,128)(2,1)} async-done(((bf16[1,384,2048]{2,1,0:T(8,128)(2,1)}), bf16[1,1536,2048]{2,1,0:T(8,128)(2,1)}) %all-gather.7.cloned.1.call-update) | async-done | bytes 6291472 | tf_op jit(solution)/shard_map/all_gather | solution.py:40
  78.8 0.6 broadcast_in_dim.21
  79.4 12.2 %fusion.3 = (bf16[1,2048,1024]{2,1,0:T(8,128)(2,1)}, f32[256,8,8,128]{3,1,2,0:T(8,128)S(1)}) fusion(pred[256,8,8,128]{3,2,1,0:T(8,128)(4,1)S(1)} %bitcast.150, bf16[1,2048,1024]{2,1,0:T(8,128)(2,1)} %param.9, bf16[1,1536,1024]{2,1,0:T(8,128)(2,1)S(1)} %copy-done, bf16[1,1536,2048]{2,1,0:T(8,128)(2,1)} %all-gather.7.cloned.1.call-done), kind=kOutput, calls=%fused_computation.7 | convolution fusion | flops 6450839552 | bytes 28311552 | tf_op jit(solution)/shard_map/dot_general | solution.py:41
  91.6 2.1 copy.13
  93.7 0.0 copy-start.5
  93.8 4.9 %copy.12 = f32[32,64,8,128]{3,1,2,0:T(8,128)} copy(f32[32,64,8,128]{3,2,1,0:T(8,128)S(1)} %bitcast.138) | data formatting | bytes 16777216 | tf_op jit(solution)/shard_map/reshape | solution.py:19
  98.6 3.9 %gather_fusion = f32[2,64,128]{2,1,0:T(8,128)S(1)} fusion(f32[256,64,128]{2,1,0:T(8,128)} %bitcast.139, s32[1024]{0:T(1024)S(1)} %pad_clamp_fusion), kind=kCustom, calls=%fused_computation | custom fusion | bytes 131080 | tf_op jit(solution)/shard_map/gather | solution.py:48
  102.6 0.7 multiply_convert_fusion
  103.3 0.0 all-gather.5.cloned.1.call-update
  104.7 0.6 dynamic-slice
  106.0 0.1 bitcast_dynamic-update-slice_fusion
  106.1 13.3 %all-reduce = s32[64]{0:T(128)S(1)} all-reduce(s32[64]{0:T(128)S(1)} %bitcast_dynamic-update-slice_fusion), channel_id=2, replica_groups=mesh['dp'=32,'tensor'=4] {'dp'}, use_global_device_ids=true, to_apply=%add | all-reduce | flops 64 | bytes 512
  119.4 27.6 %all-gather.5.cloned.1.call-done = bf16[64,64,128]{2,1,0:T(8,128)(2,1)} async-done(((bf16[2,64,128]{2,1,0:T(8,128)(2,1)}), bf16[64,64,128]{2,1,0:T(8,128)(2,1)}) %all-gather.5.cloned.1.call-update) | async-done | bytes 1048592 | tf_op jit(solution)/shard_map/all_gather | solution.py:53
  147.0 4.0 %bitcast_select_fusion = (bf16[64,64,128]{2,1,0:T(8,128)(2,1)S(1)}, bf16[64,64,128]{2,1,0:T(8,128)(2,1)S(1)}, bf16[64,64,128]{2,1,0:T(8,128)(2,1)S(1)}, bf16[64,...) fusion(bf16[64,64,128]{2,1,0:T(8,128)(2,1)} %all-gather.5.clone, ...), kind=kLoop, calls=%fused_computation.33 | loop fusion | flops 4194304 | bytes 17825800 | tf_op jit(solution)/shard_map/jit(_where)/select_n | solution.py:63
  151.1 1.3 fusion.7
  152.3 1.3 fusion.10
  153.6 4.5 %fusion.13 = f32[256,8192]{1,0:T(8,128)} fusion(bf16[8,8,64,128]{3,2,1,0:T(8,128)(2,1)S(1)} %bitcast.144, s32[64]{0:T(128)S(1)} %get-tuple-element.18), kind=kOutput, calls=%fused_computation.18 | convolution fusion | flops 268451840 | bytes 9437440 | tf_op jit(solution)/shard_map/dot_general | solution.py:66
  158.2 4.5 %fusion.16 = f32[256,8192]{1,0:T(8,128)} fusion(bf16[8,8,64,128]{3,2,1,0:T(8,128)(2,1)S(1)} %bitcast.143, s32[64]{0:T(128)S(1)} %get-tuple-element.17), kind=kOutput, calls=%fused_computation.21 | convolution fusion | flops 268451840 | bytes 9437440 | tf_op jit(solution)/shard_map/dot_general | solution.py:66
  162.7 4.5 %fusion.19 = f32[256,8192]{1,0:T(8,128)} fusion(bf16[8,8,64,128]{3,2,1,0:T(8,128)(2,1)S(1)} %bitcast.142, s32[64]{0:T(128)S(1)} %get-tuple-element.16), kind=kOutput, calls=%fused_computation.24 | convolution fusion | flops 268451840 | bytes 9437440 | tf_op jit(solution)/shard_map/dot_general | solution.py:66
  167.2 4.5 %fusion.22 = f32[256,8192]{1,0:T(8,128)} fusion(bf16[8,8,64,128]{3,2,1,0:T(8,128)(2,1)S(1)} %bitcast.141, s32[64]{0:T(128)S(1)} %get-tuple-element.15), kind=kOutput, calls=%fused_computation.27 | convolution fusion | flops 268451840 | bytes 9437440 | tf_op jit(solution)/shard_map/dot_general | solution.py:66
  171.7 4.5 %fusion.25 = f32[256,8192]{1,0:T(8,128)} fusion(bf16[8,8,64,128]{3,2,1,0:T(8,128)(2,1)S(1)} %bitcast.140, s32[64]{0:T(128)S(1)} %get-tuple-element.14), kind=kOutput, calls=%fused_computation.30 | convolution fusion | flops 268451840 | bytes 9437440 | tf_op jit(solution)/shard_map/dot_general | solution.py:66
  176.2 21.6 %divide_convert_fusion = bf16[256,8192]{1,0:T(8,128)(2,1)} fusion(f32[256,8192]{1,0:T(8,128)S(1)} %fusion.7, f32[256,8192]{1,0:T(8,128)S(1)} %fusion.10, f32[256,8192]{1,0:T(8,128)} %fusion.13, f32[256,8192]{1,0:T(8,128)} %fusion.16, f32[256,8192]{1,0:T(8,128)} %fusion.19, f32[256,8192]{1,0:T(8,128)} %fusion.22, f32[256,8192]{1,0:T(8,128)} %fusion.25, ...), kind=kOutput, calls=%fused_computation.3 | convolution fusion | flops 354435072 | bytes 63963456 | tf_op jit(solution)/shard_map/dot_general | solution.py:66
  197.8 5.4 %copy.60 = bf16[256,8,8,128]{3,1,2,0:T(8,128)(2,1)} copy(bf16[256,8,8,128]{3,2,1,0:T(8,128)(2,1)} %bitcast.148) | data formatting | bytes 8388608
  203.2 1.0 copy.64
  (13 shorter events, 0.0 us)
Async XLA Ops:
  7.2 72.3 %copy-start = (bf16[1,1536,1024]{2,1,0:T(8,128)(2,1)S(1)}, bf16[1,1536,1024]{2,1,0:T(8,128)(2,1)}, u32[]{:S(2)}) copy-start(bf16[1,1536,1024]{2,1,0:T(8,128)(2,1)} %param.8) | copy-start | bytes 9437188
  7.2 71.6 %all-gather.7.cloned.1.call-start = ((), (), s32[]{:S(2)}) async-start(), calls=%async_computation.1 | async-start | bytes 7864320 | tf_op jit(solution)/shard_map/all_gather | solution.py:40
  7.9 139.1 %all-gather.5.cloned.1.call-start = ((), (), s32[]{:S(2)}) async-start(), calls=%async_computation | async-start | bytes 1081344 | tf_op jit(solution)/shard_map/all_gather | solution.py:53
  93.7 11.0 %copy-start.5 = (u32[128]{0:T(128)S(1)}, u32[128]{0:T(128)}, u32[]{:S(2)}) copy-start(u32[128]{0:T(128)} %constant.93) | copy-start | bytes 1540
  93.7 12.3 %copy-start.4 = (s32[1,1,2]{2,1,0:T(1,128)S(1)}, s32[1,1,2]{2,1,0:T(1,128)}, u32[]{:S(2)}) copy-start(s32[1,1,2]{2,1,0:T(1,128)} %param.10) | copy-start | bytes 28
  93.8 25.7 %copy-start.3 = (s32[8,1,64]{2,1,0:T(1,128)S(1)}, s32[8,1,64]{2,1,0:T(1,128)}, u32[]{:S(2)}) copy-start(s32[8,1,64]{2,1,0:T(1,128)} %param.12) | copy-start | bytes 6148
  176.2 28.0 %copy-start.1 = (bf16[1,1536,1024]{2,1,0:T(8,128)(2,1)S(1)}, bf16[1,1536,1024]{2,1,0:T(8,128)(2,1)}, u32[]{:S(2)}) copy-start(bf16[1,1536,1024]{2,1,0:T(8,128)(2,1)} %param.8) | copy-start | bytes 9437188
  197.8 5.4 %copy-start.2 = (bf16[64,64,128]{2,1,0:T(8,128)(2,1)S(1)}, bf16[64,64,128]{2,1,0:T(8,128)(2,1)}, u32[]{:S(2)}) copy-start(bf16[64,64,128]{2,1,0:T(8,128)(2,1)} %all-gather.5.cloned.1.call-done) | copy-start | bytes 3145732
Sparse Core Ops, SparseCore 0:
  9.7 69.0 all-gather.6
  103.4 43.6 all-gather.4
where the time goes:
time: 211 us
  waiting for transfers between devices  96.8 us (46%)
  matrix products  58.9 us (28%)
  local copies, waits for them, and re-layouts  18.6 us (9%)
  between operations  16.3 us (8%)
  blocking collectives  13.3 us (6%)
  other arithmetic  6.92 us (3%)
    all_gather x1, waiting for transfers between devices, local(): gathered = lax.all_gather(token_rows, 'tensor', axis=0, tiled=True)  68.5 us
    dot_general x8, matrix products, local(): jnp.dot(onehot, values.reshape(entry_total, BH * BW), preferred_element_t...  46.7 us
    all_gather x1, waiting for transfers between devices, local(): lax.all_gather(outgoing, 'dp', axis=0, tiled=True)  27.6 us
    unnamed x1, blocking collectives  13.3 us
    dot_general x1, matrix products, local(): lax.dot_general(gathered, upstream, contract, preferred_element_type=jnp....  12.2 us
    unnamed x18, local copies, waits for them, and re-layouts  9.16 us
    reshape x1, local copies, waits for them, and re-layouts, to_blocks(): matrix.reshape(row_blocks, BH, col_blocks, BW).transpose(0, 2, 1, 3)  4.86 us
  transfers between devices with their start and end apart: 2, of which 2 were waited for; matrix products, arithmetic and copies ran while one was open for 1% of the time, Pallas kernels for 0%

commit v1 on v0

--- a/solution.py
+++ b/solution.py
@@ -10,6 +10,16 @@
 decay_first = 0.9
 decay_second = 0.999
 epsilon = 0.001
+
+
+def pass_along(array, axis, d):
+    size = lax.axis_size(axis)
+    moving, shards = (array, [array])
+    for _ in range(size - 1):
+        moving = lax.ppermute(moving, axis, [(i, (i + 1) % size) for i in range(size)])
+        shards.insert(0, moving)
+    row_of_blocks = jnp.concatenate(shards, axis=d)
+    return jnp.roll(row_of_blocks, (lax.axis_index(axis) + 1) * array.shape[d], axis=d)
 
 
 def to_blocks(matrix):
@@ -37,7 +47,7 @@
     upstream = upstream_grad[0]
     shard_width = upstream.shape[1]
     contract = (((0,), (0,)), ((), ()))
-    gathered = lax.all_gather(token_rows, "tensor", axis=0, tiled=True)
+    gathered = pass_along(token_rows, "tensor", 0)
     gradient = lax.dot_general(gathered, upstream, contract, preferred_element_type=jnp.float32)
     accumulated = gradient + feedback[0].astype(jnp.float32)
     blocks = to_blocks(accumulated)

time: 211 us -> 270 us (1.28)
  waiting for transfers between devices: 96.8 us -> 131 us
  local copies, waits for them, and re-layouts: 18.6 us -> 38.1 us
  blocking collectives: 13.3 us -> 16.4 us
    ppermute x0 -> x3, waiting for transfers between devices: none -> 105 us  [pass_along(): lax.ppermute(moving, axis, [(i, (i + 1) % size) for i in range(size)])]
    all_gather x1 -> x0, waiting for transfers between devices: 68.5 us -> none  [local(): gathered = lax.all_gather(token_rows, 'tensor', axis=0, tiled=True)]
    unnamed x18 -> x33, local copies, waits for them, and re-layouts: 9.16 us -> 27.3 us
    unnamed x1, blocking collectives: 13.3 us -> 16.4 us
  transfers between devices with their start and end apart: 2 -> 4, of which waited for: 2 -> 4; matrix products, arithmetic and copies ran while one was open for 1% -> 1% of each run, Pallas kernels for 0% -> 0%
where the time goes in v1:
time: 270 us; the launch traced here: 269 us
  waiting for transfers between devices  131 us (49%)
  matrix products  58.3 us (22%)
  local copies, waits for them, and re-layouts  38.1 us (14%)
  blocking collectives  16.4 us (6%)
  between operations  16.3 us (6%)
  other arithmetic  6.88 us (3%)
    ppermute x3, waiting for transfers between devices, pass_along(): lax.ppermute(moving, axis, [(i, (i + 1) % size) for i in range(size)])  105 us
    dot_general x8, matrix products, local(): jnp.dot(onehot, values.reshape(entry_total, BH * BW), preferred_element_t...  46.8 us
    unnamed x33, local copies, waits for them, and re-layouts  27.3 us
    all_gather x1, waiting for transfers between devices, local(): lax.all_gather(outgoing, 'dp', axis=0, tiled=True)  25.3 us
    unnamed x1, blocking collectives  16.4 us
    dot_general x1, matrix products, local(): lax.dot_general(gathered, upstream, contract, preferred_element_type=jnp....  11.5 us
  transfers between devices with their start and end apart: 4, of which 4 were waited for; matrix products, arithmetic and copies ran while one was open for 1% of the time, Pallas kernels for 0%

profile of v1, /device:TPU:1, one launch (start us, length us, event | category | flops | bytes accessed | tf_op | source)
XLA Modules:
  0.0 269.2 jit_solution(6217930498317978492)
XLA Ops:
  7.2 2.5 collective-permute-start
  9.8 36.5 %collective-permute-done = bf16[384,2048]{1,0:T(8,128)(2,1)S(1)} collective-permute-done((bf16[384,2048]{1,0:T(8,128)(2,1)}, bf16[384,2048]{1,0:T(8,128)(2,1)S(1)}, u32[]{:S(2)}, u32[]{:S(2)}) %collective-permute-start) | collective-permute-done | bytes 1572896 | tf_op jit(solution)/shard_map/ppermute | solution.py:19
  46.2 1.1 copy-done.3
  47.4 36.0 %collective-permute-done.1 = bf16[384,2048]{1,0:T(8,128)(2,1)} collective-permute-done((bf16[384,2048]{1,0:T(8,128)(2,1)S(1)}, bf16[384,2048]{1,0:T(8,128)(2,1)}, u32[]{:S(2)}, u32[]{:S(2)}) %collective-permute-start.1) | collective-permute-done | bytes 1572896 | tf_op jit(solution)/shard_map/ppermute | solution.py:19
  83.3 0.7 compare_reduce_fusion
  84.2 0.8 fusion.44
  85.6 33.0 %collective-permute-done.2 = bf16[384,2048]{1,0:T(8,128)(2,1)} collective-permute-done((bf16[384,2048]{1,0:T(8,128)(2,1)}, bf16[384,2048]{1,0:T(8,128)(2,1)}, u32[]{:S(2)}, u32[]{:S(2)}) %collective-permute-start.2) | collective-permute-done | bytes 1572896 | tf_op jit(solution)/shard_map/ppermute | solution.py:19
  118.6 2.7 %constant_dynamic-update-slice_fusion.7 = bf16[3072,2048]{1,0:T(8,128)(2,1)} fusion(bf16[384,2048]{1,0:T(8,128)(2,1)} %collective-permute-done.2), kind=kLoop, calls=%fused_computation.65 | loop fusion | bytes 3145728
  121.3 2.8 %constant_dynamic-update-slice_fusion.6 = bf16[3072,2048]{1,0:T(8,128)(2,1)} fusion(bf16[3072,2048]{1,0:T(8,128)(2,1)} %constant_dynamic-update-slice_fusion.7, bf16[384,2048]{1,0:T(8,128)(2,1)} %collective-permute-done.1), kind=kLoop, calls=%fused_computation.64 | loop fusion | bytes 3145728
  124.2 2.7 %constant_dynamic-update-slice_fusion.5 = bf16[3072,2048]{1,0:T(8,128)(2,1)} fusion(bf16[3072,2048]{1,0:T(8,128)(2,1)} %constant_dynamic-update-slice_fusion.6, bf16[384,2048]{1,0:T(8,128)(2,1)} %copy-done.3), kind=kLoop, calls=%fused_computation.63 | loop fusion | bytes 3145728
  126.9 1.3 constant_dynamic-update-slice_fusion.4
  128.2 3.3 %constant_dynamic-update-slice_fusion.3 = bf16[3072,2048]{1,0:T(8,128)(2,1)} fusion(bf16[3072,2048]{1,0:T(8,128)(2,1)} %constant_dynamic-update-slice_fusion.4, bf16[384,2048]{1,0:T(8,128)(2,1)} %collective-permute-done.2), kind=kLoop, calls=%fused_computation.61 | loop fusion | bytes 3145728
  131.5 2.8 %constant_dynamic-update-slice_fusion.2 = bf16[3072,2048]{1,0:T(8,128)(2,1)} fusion(bf16[3072,2048]{1,0:T(8,128)(2,1)} %constant_dynamic-update-slice_fusion.3, bf16[384,2048]{1,0:T(8,128)(2,1)} %collective-permute-done.1), kind=kLoop, calls=%fused_computation.60 | loop fusion | bytes 3145728
  134.3 1.3 constant_dynamic-update-slice_fusion.1
  135.6 1.3 constant_dynamic-update-slice_fusion
  137.5 11.5 %fusion.3 = (bf16[1,2048,1024]{2,1,0:T(8,128)(2,1)}, f32[256,8,8,128]{3,1,2,0:T(8,128)S(1)}) fusion(pred[256,8,8,128]{3,2,1,0:T(8,128)(4,1)S(1)} %bitcast.149, bf16[1,2048,1024]{2,1,0:T(8,128)(2,1)S(1)} %copy-done.7, bf16[1,1536,1024]{2,1,0:T(8,128)(2,1)S(1)} %copy-done, bf16[3072,2048]{1,0:T(8,128)(2,1)} %constant_dynamic-update-slice_fusion, s32[]{:T(128)S(6)} %select_n.180), kind=kOutput, calls=%fused_computation.7 | convolution fusion | flops 6450839552 | bytes 28311556 | tf_op jit(solution)/shard_map/dot_general | solution.py:51
  149.0 2.1 copy.13
  151.2 4.9 %copy.12 = f32[32,64,8,128]{3,1,2,0:T(8,128)} copy(f32[32,64,8,128]{3,2,1,0:T(8,128)S(1)} %bitcast.136) | data formatting | bytes 16777216 | tf_op jit(solution)/shard_map/reshape | solution.py:29
  156.0 3.9 %gather_fusion = f32[2,64,128]{2,1,0:T(8,128)S(1)} fusion(f32[256,64,128]{2,1,0:T(8,128)} %bitcast.137, s32[1024]{0:T(1024)S(1)} %pad_clamp_fusion), kind=kCustom, calls=%fused_computation | custom fusion | bytes 131080 | tf_op jit(solution)/shard_map/gather | solution.py:58
  163.5 16.4 %all-reduce = s32[64]{0:T(128)S(1)} all-reduce(s32[64]{0:T(128)S(1)} %bitcast_dynamic-update-slice_fusion), channel_id=2, replica_groups=mesh['dp'=32,'tensor'=4] {'dp'}, use_global_device_ids=true, to_apply=%add | all-reduce | flops 64 | bytes 512
  180.0 25.3 %all-gather.3.cloned.1.call-done = bf16[64,64,128]{2,1,0:T(8,128)(2,1)} async-done(((bf16[2,64,128]{2,1,0:T(8,128)(2,1)}), bf16[64,64,128]{2,1,0:T(8,128)(2,1)}) %all-gather.3.cloned.1.call-update) | async-done | bytes 1048592 | tf_op jit(solution)/shard_map/all_gather | solution.py:63
  205.2 4.0 %bitcast_select_fusion = (bf16[64,64,128]{2,1,0:T(8,128)(2,1)S(1)}, bf16[64,64,128]{2,1,0:T(8,128)(2,1)S(1)}, bf16[64,64,128]{2,1,0:T(8,128)(2,1)S(1)}, bf16[64,...) fusion(bf16[64,64,128]{2,1,0:T(8,128)(2,1)} %all-gather.3.clone, ...), kind=kLoop, calls=%fused_computation.33 | loop fusion | flops 4194304 | bytes 17825800 | tf_op jit(solution)/shard_map/jit(_where)/select_n | solution.py:73
  209.2 1.3 fusion.7
  210.5 1.3 fusion.10
  211.8 4.5 %fusion.13 = f32[256,8192]{1,0:T(8,128)} fusion(bf16[8,8,64,128]{3,2,1,0:T(8,128)(2,1)S(1)} %bitcast.143, s32[64]{0:T(128)S(1)} %get-tuple-element.18), kind=kOutput, calls=%fused_computation.18 | convolution fusion | flops 268451840 | bytes 9437440 | tf_op jit(solution)/shard_map/dot_general | solution.py:76
  216.3 4.5 %fusion.16 = f32[256,8192]{1,0:T(8,128)} fusion(bf16[8,8,64,128]{3,2,1,0:T(8,128)(2,1)S(1)} %bitcast.142, s32[64]{0:T(128)S(1)} %get-tuple-element.17), kind=kOutput, calls=%fused_computation.21 | convolution fusion | flops 268451840 | bytes 9437440 | tf_op jit(solution)/shard_map/dot_general | solution.py:76
  220.8 4.5 %fusion.19 = f32[256,8192]{1,0:T(8,128)} fusion(bf16[8,8,64,128]{3,2,1,0:T(8,128)(2,1)S(1)} %bitcast.141, s32[64]{0:T(128)S(1)} %get-tuple-element.16), kind=kOutput, calls=%fused_computation.24 | convolution fusion | flops 268451840 | bytes 9437440 | tf_op jit(solution)/shard_map/dot_general | solution.py:76
  225.4 4.5 %fusion.22 = f32[256,8192]{1,0:T(8,128)} fusion(bf16[8,8,64,128]{3,2,1,0:T(8,128)(2,1)S(1)} %bitcast.140, s32[64]{0:T(128)S(1)} %get-tuple-element.15), kind=kOutput, calls=%fused_computation.27 | convolution fusion | flops 268451840 | bytes 9437440 | tf_op jit(solution)/shard_map/dot_general | solution.py:76
  229.9 4.5 %fusion.25 = f32[256,8192]{1,0:T(8,128)} fusion(bf16[8,8,64,128]{3,2,1,0:T(8,128)(2,1)S(1)} %bitcast.139, s32[64]{0:T(128)S(1)} %get-tuple-element.14), kind=kOutput, calls=%fused_computation.30 | convolution fusion | flops 268451840 | bytes 9437440 | tf_op jit(solution)/shard_map/dot_general | solution.py:76
  234.4 21.7 %divide_convert_fusion = bf16[256,8192]{1,0:T(8,128)(2,1)} fusion(f32[256,8192]{1,0:T(8,128)S(1)} %fusion.7, f32[256,8192]{1,0:T(8,128)S(1)} %fusion.10, f32[256,8192]{1,0:T(8,128)} %fusion.13, f32[256,8192]{1,0:T(8,128)} %fusion.16, f32[256,8192]{1,0:T(8,128)} %fusion.19, f32[256,8192]{1,0:T(8,128)} %fusion.22, f32[256,8192]{1,0:T(8,128)} %fusion.25, ...), kind=kOutput, calls=%fused_computation.3 | convolution fusion | flops 354435072 | bytes 63963456 | tf_op jit(solution)/shard_map/dot_general | solution.py:76
  256.0 5.4 %copy.60 = bf16[256,8,8,128]{3,1,2,0:T(8,128)(2,1)} copy(bf16[256,8,8,128]{3,2,1,0:T(8,128)(2,1)} %bitcast.147) | data formatting | bytes 8388608
  261.4 1.0 copy.71
  (32 shorter events, 2.9 us)
Async XLA Ops:
  7.2 130.3 %copy-start = (bf16[1,1536,1024]{2,1,0:T(8,128)(2,1)S(1)}, bf16[1,1536,1024]{2,1,0:T(8,128)(2,1)}, u32[]{:S(2)}) copy-start(bf16[1,1536,1024]{2,1,0:T(8,128)(2,1)} %param.8) | copy-start | bytes 9437188
  7.2 198.1 %all-gather.3.cloned.1.call-start = ((), (), s32[]{:S(2)}) async-start(), calls=%async_computation | async-start | bytes 1081344 | tf_op jit(solution)/shard_map/all_gather | solution.py:63
  7.2 39.0 %collective-permute-start = (bf16[384,2048]{1,0:T(8,128)(2,1)}, bf16[384,2048]{1,0:T(8,128)(2,1)S(1)}, u32[]{:S(2)}, u32[]{:S(2)}) collective-permute-start(bf16[384,2048]{1,0:T(8,128)(2,1)} %bitcast.138), channel_id=1, source_target_pairs={{0,1},{1,2},{2,3},{3,0},{4,5},{5,6},{6,7},{7,4},{8,9},{9,10},{10,1... | collective-permute-start | bytes 4718600 | tf_op jit(solution)/shard_map/ppermute | solution.py:19
  46.2 1.1 copy-start.3
  47.4 36.0 %collective-permute-start.1 = (bf16[384,2048]{1,0:T(8,128)(2,1)S(1)}, bf16[384,2048]{1,0:T(8,128)(2,1)}, u32[]{:S(2)}, u32[]{:S(2)}) collective-permute-start(bf16[384,2048]{1,0:T(8,128)(2,1)S(1)} %collective-permute-done), channel_id=1, source_target_pairs={{0,1},{1,2},{2,3},{3,0},{4,5},{5,6},{6,7},{7,4},{8,9},{9,10},{10,1... | collective-permute-start | bytes 4718600 | tf_op jit(solution)/shard_map/ppermute | solution.py:19
  83.3 35.3 %collective-permute-start.2 = (bf16[384,2048]{1,0:T(8,128)(2,1)}, bf16[384,2048]{1,0:T(8,128)(2,1)}, u32[]{:S(2)}, u32[]{:S(2)}) collective-permute-start(bf16[384,2048]{1,0:T(8,128)(2,1)} %collective-permute-done.1), channel_id=1, source_target_pairs={{0,1},{1,2},{2,3},{3,0},{4,5},{5,6},{6,7},{7,4},{8,9},{9,10},{10,1... | collective-permute-start | bytes 4718600 | tf_op jit(solution)/shard_map/ppermute | solution.py:19
  84.2 42.8 %copy-start.2 = (bf16[1,384,2048]{2,1,0:T(8,128)(2,1)S(1)}, bf16[1,384,2048]{2,1,0:T(8,128)(2,1)}, u32[]{:S(2)}) copy-start(bf16[1,384,2048]{2,1,0:T(8,128)(2,1)} %param.7) | copy-start | bytes 4718596
  121.3 13.0 %copy-start.4 = (bf16[384,2048]{1,0:T(8,128)(2,1)S(1)}, bf16[384,2048]{1,0:T(8,128)(2,1)}, u32[]{:S(2)}) copy-start(bf16[384,2048]{1,0:T(8,128)(2,1)} %copy-done.3) | copy-start | bytes 4718596
  126.9 10.6 %copy-start.7 = (bf16[1,2048,1024]{2,1,0:T(8,128)(2,1)S(1)}, bf16[1,2048,1024]{2,1,0:T(8,128)(2,1)}, u32[]{:S(2)}) copy-start(bf16[1,2048,1024]{2,1,0:T(8,128)(2,1)} %param.9) | copy-start | bytes 12582916
  151.1 11.0 %copy-start.9 = (u32[128]{0:T(128)S(1)}, u32[128]{0:T(128)}, u32[]{:S(2)}) copy-start(u32[128]{0:T(128)} %constant.117) | copy-start | bytes 1540
  151.1 12.3 %copy-start.8 = (s32[1,1,2]{2,1,0:T(1,128)S(1)}, s32[1,1,2]{2,1,0:T(1,128)}, u32[]{:S(2)}) copy-start(s32[1,1,2]{2,1,0:T(1,128)} %param.10) | copy-start | bytes 28
  151.2 28.8 %copy-start.6 = (s32[8,1,64]{2,1,0:T(1,128)S(1)}, s32[8,1,64]{2,1,0:T(1,128)}, u32[]{:S(2)}) copy-start(s32[8,1,64]{2,1,0:T(1,128)} %param.12) | copy-start | bytes 6148
  234.4 28.0 %copy-start.1 = (bf16[1,1536,1024]{2,1,0:T(8,128)(2,1)S(1)}, bf16[1,1536,1024]{2,1,0:T(8,128)(2,1)}, u32[]{:S(2)}) copy-start(bf16[1,1536,1024]{2,1,0:T(8,128)(2,1)} %param.8) | copy-start | bytes 9437188
  256.0 5.4 %copy-start.5 = (bf16[64,64,128]{2,1,0:T(8,128)(2,1)S(1)}, bf16[64,64,128]{2,1,0:T(8,128)(2,1)}, u32[]{:S(2)}) copy-start(bf16[64,64,128]{2,1,0:T(8,128)(2,1)} %all-gather.3.cloned.1.call-done) | copy-start | bytes 3145732
Sparse Core Ops, SparseCore 0:
  160.8 44.3 all-gather.2
